TPU v7x, 256 devices: a whole 4x4x8 slice. The times are simulated.
256 devices in a mesh: dp: 8 (over y, core), ctx: 32 (over x, z).
Axes of the slice: x: 4, y: 4, z: 8, core: 2. Of those that a mesh axis runs over, the one named last changes fastest.
Arguments:
- features: bfloat16 [8, 4096, 1536], P('dp', 'ctx'), may hold values from -6 to 6
- short_weight: float32 [7, 1536], replicated, may hold values from -2 to 2
- long_filter: float32 [4096, 512], P('ctx'), may hold values from -4 to 4
- skip_bias: float32 [512], replicated, may hold values from 0.5 to 1.5
- cotangent: bfloat16 [8, 4096, 512], P('dp', 'ctx'), may hold values from -6 to 6
Outputs:
- layer_out: bfloat16 [8, 4096, 512], P('dp', 'ctx')
- grad_features: bfloat16 [8, 4096, 1536], P('dp', 'ctx')
- grad_short: float32 [7, 1536], replicated
- grad_filter: float32 [4096, 512], P('ctx')
- grad_skip: float32 [512], replicated
All inputs are finite; a program needn't handle non-finite values.
Results may differ from a plain program's by a relative error of at most 0.001.
Values may be sent and summed in bfloat16 or wider, within the bound.
A program may use at most 64 MiB of HBM per device.

v0:
```python
import math
import jax
import jax.numpy as jnp
from jax import lax
from jax.sharding import PartitionSpec as P

PRECISE = lax.Precision.HIGHEST


def swapped(value, axis, distance):
    mask = 2**distance
    pairs = [(source, source ^ mask) for source in range(lax.axis_size(axis))]
    return lax.ppermute(value, axis, pairs)


def shifted(value, axis, steps):
    count = lax.axis_size(axis)
    initial, last = (max(0, -steps), min(count, count - steps))
    return lax.ppermute(value, axis, [(source, source + steps) for source in range(initial, last)])


def bit_reverse(index_value, bit_count):
    reversed_value = jnp.zeros_like(index_value)
    for bit_place in range(bit_count):
        digit_now = index_value // 2**bit_place % 2
        reversed_value = reversed_value + digit_now * 2 ** (bit_count - 1 - bit_place)
    return reversed_value


def spectral_table(device, parts_count, tokens):
    bit_count = parts_count.bit_length() - 1
    coarse_freq = 2 * bit_reverse(device, bit_count) + jnp.arange(2, dtype=jnp.int32)
    total_points = 2 * parts_count * tokens
    column_index = jnp.arange(tokens, dtype=jnp.int32)
    full_freq = coarse_freq[:, None] + 2 * parts_count * column_index[None, :]
    phase_value = column_index[None, None, :] * full_freq[:, :, None] % total_points
    angle_value = phase_value.astype(jnp.float32) * (2.0 * math.pi / total_points)
    return (jnp.cos(angle_value), -jnp.sin(angle_value))


def contract(matrix, values):
    return jnp.einsum("akm,amw->akw", matrix, values, precision=PRECISE)


def contract_back(matrix, values):
    return jnp.einsum("akm,akw->amw", matrix, values, precision=PRECISE)


def local_forward(spec_real, spec_imag, table):
    table_real, table_imag = table
    out_real = contract(table_real, spec_real) - contract(table_imag, spec_imag)
    out_imag = contract(table_real, spec_imag) + contract(table_imag, spec_real)
    return (out_real, out_imag)


def local_inverse(spec_real, spec_imag, table):
    table_real, table_imag = table
    factor = 1.0 / spec_real.shape[1]
    out_real = (
        contract_back(table_real, spec_real) + contract_back(table_imag, spec_imag)
    ) * factor
    out_imag = (
        contract_back(table_real, spec_imag) - contract_back(table_imag, spec_real)
    ) * factor
    return (out_real, out_imag)


def pair_swap(stacked, bit_place):
    return swapped(stacked, "ctx", bit_place)


def pair_swap_back(stacked, bit_place):
    return swapped(stacked, "ctx", bit_place)


def section_terms(device, bit_place):
    span_size = 2**bit_place
    upper_flag = device // span_size % 2
    sign_value = (1 - 2 * upper_flag).astype(jnp.float32)
    turn_value = math.pi / span_size * (upper_flag * (device % span_size)).astype(jnp.float32)
    return (sign_value, jnp.cos(turn_value), jnp.sin(turn_value))


def butterfly_forward(signals):
    parts_count = lax.axis_size("ctx")
    device = lax.axis_index("ctx")
    bit_count = parts_count.bit_length() - 1
    angle_value = math.pi * device.astype(jnp.float32) / parts_count
    spec_real = jnp.stack([signals, signals * jnp.cos(angle_value)])
    spec_imag = jnp.stack([jnp.zeros_like(signals), -signals * jnp.sin(angle_value)])
    for bit_place in reversed(range(bit_count)):
        sign_value, cos_turn, sin_turn = section_terms(device, bit_place)
        partner = pair_swap(jnp.stack([spec_real, spec_imag]), bit_place)
        joined_real = partner[0] + sign_value * spec_real
        joined_imag = partner[1] + sign_value * spec_imag
        spec_real = joined_real * cos_turn + joined_imag * sin_turn
        spec_imag = joined_imag * cos_turn - joined_real * sin_turn
    return (spec_real, spec_imag)


def butterfly_inverse(spec_real, spec_imag):
    parts_count = lax.axis_size("ctx")
    device = lax.axis_index("ctx")
    bit_count = parts_count.bit_length() - 1
    for bit_place in range(bit_count):
        sign_value, cos_turn, sin_turn = section_terms(device, bit_place)
        turned_real = spec_real * cos_turn - spec_imag * sin_turn
        turned_imag = spec_imag * cos_turn + spec_real * sin_turn
        partner = pair_swap_back(jnp.stack([turned_real, turned_imag]), bit_place)
        spec_real = 0.5 * (partner[0] + sign_value * turned_real)
        spec_imag = 0.5 * (partner[1] + sign_value * turned_imag)
    angle_value = math.pi * device.astype(jnp.float32) / parts_count
    cos_last = jnp.cos(angle_value)
    sin_last = jnp.sin(angle_value)
    out_real = 0.5 * (spec_real[0] + spec_real[1] * cos_last - spec_imag[1] * sin_last)
    out_imag = 0.5 * (spec_imag[0] + spec_imag[1] * cos_last + spec_real[1] * sin_last)
    return (out_real, out_imag)


def per_device(features, short_weight, long_filter, skip_bias, cotangent):
    taps = short_weight.shape[0]
    token_rows = features[0]
    tokens = token_rows.shape[0]
    channels = long_filter.shape[1]
    parts_count = lax.axis_size("ctx")
    device = lax.axis_index("ctx")
    history = shifted(token_rows[tokens - (taps - 1) :], "ctx", 1)
    extended = jnp.concatenate([history, token_rows], axis=0).astype(jnp.float32)
    mixed_feats = jnp.zeros((tokens, token_rows.shape[1]), jnp.float32)
    for tap_index in range(taps):
        start_row = taps - 1 - tap_index
        mixed_feats = (
            mixed_feats + short_weight[tap_index] * extended[start_row : start_row + tokens]
        )
    query = mixed_feats[:, :channels]
    key_part = mixed_feats[:, channels : 2 * channels]
    value_part = mixed_feats[:, 2 * channels :]
    gated = key_part * value_part
    upstream = cotangent[0].astype(jnp.float32)
    dconv = upstream * query
    signals = jnp.concatenate([gated, long_filter, dconv], axis=1)
    table = spectral_table(device, parts_count, tokens)
    spec_real, spec_imag = butterfly_forward(signals)
    spec_real, spec_imag = local_forward(spec_real, spec_imag, table)
    gated_real = spec_real[..., :channels]
    gated_imag = spec_imag[..., :channels]
    filter_real = spec_real[..., channels : 2 * channels]
    filter_imag = spec_imag[..., channels : 2 * channels]
    dconv_real = spec_real[..., 2 * channels :]
    dconv_imag = spec_imag[..., 2 * channels :]
    conv_real = gated_real * filter_real - gated_imag * filter_imag
    conv_imag = gated_real * filter_imag + gated_imag * filter_real
    back_real = filter_real * dconv_real + filter_imag * dconv_imag
    back_imag = filter_real * dconv_imag - filter_imag * dconv_real
    corr_real = gated_real * dconv_real + gated_imag * dconv_imag
    corr_imag = gated_real * dconv_imag - gated_imag * dconv_real
    inverse_real = jnp.concatenate([conv_real - back_imag, corr_real], axis=-1)
    inverse_imag = jnp.concatenate([conv_imag + back_real, corr_imag], axis=-1)
    inverse_real, inverse_imag = local_inverse(inverse_real, inverse_imag, table)
    result_real, result_imag = butterfly_inverse(inverse_real, inverse_imag)
    long_conv = result_real[:, :channels] + skip_bias * gated
    dgated = result_imag[:, :channels] + skip_bias * dconv
    filter_part = result_real[:, channels:]
    layer_out = (query * long_conv).astype(jnp.bfloat16)[None]
    dmixed = jnp.concatenate([upstream * long_conv, dgated * value_part, dgated * key_part], axis=1)
    later = shifted(dmixed[: taps - 1], "ctx", -1)
    ahead = jnp.concatenate([dmixed, later], axis=0)
    grad_local = jnp.zeros_like(dmixed)
    short_rows = []
    for tap_index in range(taps):
        grad_local = grad_local + short_weight[tap_index] * ahead[tap_index : tap_index + tokens]
        start_row = taps - 1 - tap_index
        short_rows.append(jnp.sum(dmixed * extended[start_row : start_row + tokens], axis=0))
    grad_features = grad_local.astype(jnp.bfloat16)[None]
    short_part = jnp.stack(short_rows)
    skip_part = jnp.sum(dconv * gated, axis=0)
    scale = 1.0 / math.sqrt(lax.axis_size("dp") * parts_count * tokens)
    filter_sum = lax.psum(filter_part, "dp")
    short_sum, skip_sum = lax.psum((short_part, skip_part), ("dp", "ctx"))
    return (layer_out, grad_features, short_sum * scale, filter_sum * scale, skip_sum * scale)


def solution(mesh):
    return jax.shard_map(
        per_device,
        mesh=mesh,
        in_specs=(P("dp", "ctx", None), P(), P("ctx", None), P(), P("dp", "ctx", None)),
        out_specs=(P("dp", "ctx", None), P("dp", "ctx", None), P(), P("ctx", None), P()),
        check_vma=False,
    )
```

profile of v0, /device:TPU:2, one launch (start us, length us, event | category | flops | bytes accessed | tf_op | source)
XLA Modules:
  0.0 1050.0 jit_solution(7923902592177502704)
XLA Ops:
  8.0 3.8 collective-permute-start
  13.2 4.3 collective-permute-done
  23.9 2.4 collective-permute-start.1
  26.5 68.2 %collective-permute-done.1 = f32[2,2,128,1536]{3,2,1,0:T(8,128)} collective-permute-done((f32[2,2,128,1536]{3,2,1,0:T(8,128)}, f32[2,2,128,1536]{3,2,1,0:T(8,128)}, u32[]{:S(2)}, u32[]{:S(2)}) %collective-permute-start.1) | collective-permute-done | bytes 3145760 | tf_op jit(solution)/shard_map/ppermute | solution.py:13
  94.7 3.0 multiply_subtract_fusion.4
  97.7 2.0 pad_maximum_fusion.1
  100.3 67.9 %collective-permute-done.2 = f32[2,2,128,1536]{3,2,1,0:T(8,128)} collective-permute-done((f32[2,2,128,1536]{3,2,1,0:T(8,128)}, f32[2,2,128,1536]{3,2,1,0:T(8,128)}, u32[]{:S(2)}, u32[]{:S(2)}) %collective-permute-start.2) | collective-permute-done | bytes 3145760 | tf_op jit(solution)/shard_map/ppermute | solution.py:13
  168.2 3.1 multiply_subtract_fusion.3
  171.3 2.1 pad_maximum_fusion.2
  174.0 4.0 collective-permute-start.3
  178.1 135.4 %collective-permute-done.3 = f32[2,2,128,1536]{3,2,1,0:T(8,128)} collective-permute-done((f32[2,2,128,1536]{3,2,1,0:T(8,128)}, f32[2,2,128,1536]{3,2,1,0:T(8,128)}, u32[]{:S(2)}, u32[]{:S(2)}) %collective-permute-start.3) | collective-permute-done | bytes 3145760 | tf_op jit(solution)/shard_map/ppermute | solution.py:13
  313.5 3.6 multiply_subtract_fusion.2
  317.1 2.1 pad_maximum_fusion.3
  319.4 137.3 %collective-permute-done.4 = f32[2,2,128,1536]{3,2,1,0:T(8,128)} collective-permute-done((f32[2,2,128,1536]{3,2,1,0:T(8,128)}, f32[2,2,128,1536]{3,2,1,0:T(8,128)}, u32[]{:S(2)}, u32[]{:S(2)}) %collective-permute-start.4) | collective-permute-done | bytes 3145760 | tf_op jit(solution)/shard_map/ppermute | solution.py:13
  456.7 3.1 multiply_add_fusion.1
  462.6 69.4 %collective-permute-done.5 = f32[2,2,128,1536]{3,2,1,0:T(8,128)} collective-permute-done((f32[2,2,128,1536]{3,2,1,0:T(8,128)}, f32[2,2,128,1536]{3,2,1,0:T(8,128)}, u32[]{:S(2)}, u32[]{:S(2)}) %collective-permute-start.5) | collective-permute-done | bytes 3145760 | tf_op jit(solution)/shard_map/ppermute | solution.py:13
  532.0 3.5 fusion.2
  552.4 45.8 %collective-permute-done.6 = f32[2,2,128,1024]{3,2,1,0:T(8,128)} collective-permute-done((f32[2,2,128,1024]{3,2,1,0:T(8,128)}, f32[2,2,128,1024]{3,2,1,0:T(8,128)}, u32[]{:S(2)}, u32[]{:S(2)}) %collective-permute-start.6) | collective-permute-done | bytes 2097184 | tf_op jit(solution)/shard_map/ppermute | solution.py:13
  598.2 2.0 multiply_add_fusion.8
  602.7 2.1 collective-permute-start.7
  604.8 89.6 %collective-permute-done.7 = f32[2,2,128,1024]{3,2,1,0:T(8,128)} collective-permute-done((f32[2,2,128,1024]{3,2,1,0:T(8,128)}, f32[2,2,128,1024]{3,2,1,0:T(8,128)}, u32[]{:S(2)}, u32[]{:S(2)}) %collective-permute-start.7) | collective-permute-done | bytes 2097184 | tf_op jit(solution)/shard_map/ppermute | solution.py:13
  694.5 2.3 multiply_add_fusion.7
  698.1 3.7 collective-permute-start.8
  701.8 92.3 %collective-permute-done.8 = f32[2,2,128,1024]{3,2,1,0:T(8,128)} collective-permute-done((f32[2,2,128,1024]{3,2,1,0:T(8,128)S(1)}, f32[2,2,128,1024]{3,2,1,0:T(8,128)}, u32[]{:S(2)}, u32[]{:S(2)}) %collective-permute-start.8) | collective-permute-done | bytes 2097184 | tf_op jit(solution)/shard_map/ppermute | solution.py:13
  794.1 2.7 multiply_add_fusion.6
  799.2 46.3 %collective-permute-done.9 = f32[2,2,128,1024]{3,2,1,0:T(8,128)} collective-permute-done((f32[2,2,128,1024]{3,2,1,0:T(8,128)}, f32[2,2,128,1024]{3,2,1,0:T(8,128)}, u32[]{:S(2)}, u32[]{:S(2)}) %collective-permute-start.9) | collective-permute-done | bytes 2097184 | tf_op jit(solution)/shard_map/ppermute | solution.py:13
  845.5 2.0 multiply_subtract_fusion.5
  847.8 3.2 collective-permute-start.10
  851.0 45.0 %collective-permute-done.10 = f32[2,2,128,1024]{3,2,1,0:T(8,128)S(1)} collective-permute-done((f32[2,2,128,1024]{3,2,1,0:T(8,128)S(1)}, f32[2,2,128,1024]{3,2,1,0:T(8,128)S(1)}, u32[]{:S(2)}, u32[]{:S(2)}) %collective-permute-start.10) | collective-permute-done | bytes 2097184 | tf_op jit(solution)/shard_map/ppermute | solution.py:13
  899.7 75.3 %all-reduce.1 = (f32[7,1536]{1,0:T(8,128)S(1)}, f32[512]{0:T(512)S(1)}) all-reduce(f32[7,1536]{1,0:T(8,128)S(1)} %stack.165, f32[512]{0:T(512)S(1)} %get-tuple-element.21), channel_id=1, replica_groups=mesh['dp'=8,'ctx'=32] {'dp','ctx'}, use_global_device_ids=true, to_apply=%region_7.8 | all-reduce | flops 11264 | bytes 90112 | tf_op jit(solution)/shard_map/psum | solution.py:179
  975.7 4.7 collective-permute-start.11
  983.7 57.8 %all-reduce.4.cloned.1.call-done = f32[128,512]{1,0:T(8,128)} async-done(((f32[128,512]{1,0:T(8,128)}), f32[128,512]{1,0:T(8,128)}) %all-reduce.4.cloned.1.call-update) | async-done | bytes 262160 | tf_op jit(solution)/shard_map/psum | solution.py:178
  (94 shorter events, 44.5 us)
Async XLA Ops:
  7.2 1034.3 %all-reduce.4.cloned.1.call-start = ((), (), s32[]{:S(2)}) async-start(), calls=%async_computation | async-start | bytes 524288 | tf_op jit(solution)/shard_map/psum | solution.py:178
  8.0 9.5 collective-permute-start
  18.6 0.9 copy-start.16
  19.5 1.4 copy-start.9
  19.5 1.1 copy-start.15
  19.6 1.3 copy-start.13
  20.9 0.9 copy-start.11
  20.9 1.1 copy-start.12
  23.9 70.8 %collective-permute-start.1 = (f32[2,2,128,1536]{3,2,1,0:T(8,128)}, f32[2,2,128,1536]{3,2,1,0:T(8,128)}, u32[]{:S(2)}, u32[]{:S(2)}) collective-permute-start(f32[2,2,128,1536]{3,2,1,0:T(8,128)} %pad_maximum_fusion), channel_id=1, source_target_pairs={{0,16},{1,17},{2,18},{3,19},{4,20},{5,21},{6,22},{7,23},{8,24},{9,... | collective-permute-start | bytes 9437192 | tf_op jit(solution)/shard_map/ppermute | solution.py:13
  97.7 2.1 copy-start.1
  99.8 68.4 %collective-permute-start.2 = (f32[2,2,128,1536]{3,2,1,0:T(8,128)}, f32[2,2,128,1536]{3,2,1,0:T(8,128)}, u32[]{:S(2)}, u32[]{:S(2)}) collective-permute-start(f32[2,2,128,1536]{3,2,1,0:T(8,128)} %pad_maximum_fusion.1), channel_id=1, source_target_pairs={{0,8},{1,9},{2,10},{3,11},{4,12},{5,13},{6,14},{7,15},{8,0},{9,1},... | collective-permute-start | bytes 9437192 | tf_op jit(solution)/shard_map/ppermute | solution.py:13
  171.3 2.3 copy-start.2
  171.3 2.7 copy-start.3
  174.0 139.6 %collective-permute-start.3 = (f32[2,2,128,1536]{3,2,1,0:T(8,128)}, f32[2,2,128,1536]{3,2,1,0:T(8,128)}, u32[]{:S(2)}, u32[]{:S(2)}) collective-permute-start(f32[2,2,128,1536]{3,2,1,0:T(8,128)} %pad_maximum_fusion.2), channel_id=1, source_target_pairs={{0,4},{1,5},{2,6},{3,7},{4,0},{5,1},{6,2},{7,3},{8,12},{9,13},{10,... | collective-permute-start | bytes 9437192 | tf_op jit(solution)/shard_map/ppermute | solution.py:13
  317.1 2.1 copy-start
  319.3 137.4 %collective-permute-start.4 = (f32[2,2,128,1536]{3,2,1,0:T(8,128)}, f32[2,2,128,1536]{3,2,1,0:T(8,128)}, u32[]{:S(2)}, u32[]{:S(2)}) collective-permute-start(f32[2,2,128,1536]{3,2,1,0:T(8,128)} %pad_maximum_fusion.3), channel_id=1, source_target_pairs={{0,2},{1,3},{2,0},{3,1},{4,6},{5,7},{6,4},{7,5},{8,10},{9,11},{10,... | collective-permute-start | bytes 9437192 | tf_op jit(solution)/shard_map/ppermute | solution.py:13
  459.8 2.1 copy-start.4
  459.8 2.7 copy-start.5
  462.5 69.5 %collective-permute-start.5 = (f32[2,2,128,1536]{3,2,1,0:T(8,128)}, f32[2,2,128,1536]{3,2,1,0:T(8,128)}, u32[]{:S(2)}, u32[]{:S(2)}) collective-permute-start(f32[2,2,128,1536]{3,2,1,0:T(8,128)} %pad_maximum_fusion.4), channel_id=1, source_target_pairs={{0,1},{1,0},{2,3},{3,2},{4,5},{5,4},{6,7},{7,6},{8,9},{9,8},{10,11... | collective-permute-start | bytes 9437192 | tf_op jit(solution)/shard_map/ppermute | solution.py:13
  552.1 46.1 %collective-permute-start.6 = (f32[2,2,128,1024]{3,2,1,0:T(8,128)}, f32[2,2,128,1024]{3,2,1,0:T(8,128)}, u32[]{:S(2)}, u32[]{:S(2)}) collective-permute-start(f32[2,2,128,1024]{3,2,1,0:T(8,128)} %pad_maximum_fusion.5), channel_id=1, source_target_pairs={{0,1},{1,0},{2,3},{3,2},{4,5},{5,4},{6,7},{7,6},{8,9},{9,8},{10,11... | collective-permute-start | bytes 6291464 | tf_op jit(solution)/shard_map/ppermute | solution.py:13
  600.3 1.0 copy-start.6
  602.7 91.7 %collective-permute-start.7 = (f32[2,2,128,1024]{3,2,1,0:T(8,128)}, f32[2,2,128,1024]{3,2,1,0:T(8,128)}, u32[]{:S(2)}, u32[]{:S(2)}) collective-permute-start(f32[2,2,128,1024]{3,2,1,0:T(8,128)} %pad_maximum_fusion.6), channel_id=1, source_target_pairs={{0,2},{1,3},{2,0},{3,1},{4,6},{5,7},{6,4},{7,5},{8,10},{9,11},{10,... | collective-permute-start | bytes 6291464 | tf_op jit(solution)/shard_map/ppermute | solution.py:13
  696.8 1.0 copy-start.7
  696.8 1.3 copy-start.8
  698.1 96.0 %collective-permute-start.8 = (f32[2,2,128,1024]{3,2,1,0:T(8,128)S(1)}, f32[2,2,128,1024]{3,2,1,0:T(8,128)}, u32[]{:S(2)}, u32[]{:S(2)}) collective-permute-start(f32[2,2,128,1024]{3,2,1,0:T(8,128)S(1)} %pad_maximum_fusion.7), channel_id=1, source_target_pairs={{0,4},{1,5},{2,6},{3,7},{4,0},{5,1},{6,2},{7,3},{8,12},{9,13},{10,... | collective-permute-start | bytes 6291464 | tf_op jit(solution)/shard_map/ppermute | solution.py:13
  798.3 47.3 %collective-permute-start.9 = (f32[2,2,128,1024]{3,2,1,0:T(8,128)}, f32[2,2,128,1024]{3,2,1,0:T(8,128)}, u32[]{:S(2)}, u32[]{:S(2)}) collective-permute-start(f32[2,2,128,1024]{3,2,1,0:T(8,128)} %pad_maximum_fusion.8), channel_id=1, source_target_pairs={{0,8},{1,9},{2,10},{3,11},{4,12},{5,13},{6,14},{7,15},{8,0},{9,1},... | collective-permute-start | bytes 6291464 | tf_op jit(solution)/shard_map/ppermute | solution.py:13
  847.8 48.2 %collective-permute-start.10 = (f32[2,2,128,1024]{3,2,1,0:T(8,128)S(1)}, f32[2,2,128,1024]{3,2,1,0:T(8,128)S(1)}, u32[]{:S(2)}, u32[]{:S(2)}) collective-permute-start(f32[2,2,128,1024]{3,2,1,0:T(8,128)S(1)} %pad_maximum_fusion.9), channel_id=1, source_target_pairs={{0,16},{1,17},{2,18},{3,19},{4,20},{5,21},{6,22},{7,23},{8,24},{9,... | collective-permute-start | bytes 6291464 | tf_op jit(solution)/shard_map/ppermute | solution.py:13
  896.6 1.1 copy-start.10
  896.6 1.2 copy-start.14
  896.6 1.2 copy-start.17
  896.7 1.2 copy-start.18
  975.7 6.5 collective-permute-start.11
Sparse Core Ops, SparseCore 0:
  981.2 60.1 all-reduce.3
where the time goes:
time: 1050 us
  waiting for transfers between devices  860 us (82%)
  blocking collectives  75.3 us (7%)
  other arithmetic  50.7 us (5%)
  starting transfers between devices  25.6 us (2%)
  between operations  15.3 us (1%)
  matrix products  14.2 us (1%)
    ppermute x10, waiting for transfers between devices, swapped(): return lax.ppermute(value, axis, pairs)  797 us
    psum x1, blocking collectives, per_device(): short_sum, skip_sum = lax.psum((short_part, skip_part), ('dp', 'ctx'))  75.3 us
    psum x1, waiting for transfers between devices, per_device(): filter_sum = lax.psum(filter_part, 'dp')  57.8 us
  transfers between devices with their start and end apart: 13, of which 13 were waited for; matrix products, arithmetic and copies ran while one was open for 0% of the time, Pallas kernels for 0%

commit v1 on v0

--- a/solution.py
+++ b/solution.py
@@ -176,7 +176,7 @@
     skip_part = jnp.sum(dconv * gated, axis=0)
     scale = 1.0 / math.sqrt(lax.axis_size("dp") * parts_count * tokens)
     filter_sum = lax.psum(filter_part, "dp")
-    short_sum, skip_sum = lax.psum((short_part, skip_part), ("dp", "ctx"))
+    short_sum, skip_sum = lax.psum(lax.psum((short_part, skip_part), "dp"), "ctx")
     return (layer_out, grad_features, short_sum * scale, filter_sum * scale, skip_sum * scale)
 
 

time: 1050 us -> 1140 us (1.086)
  blocking collectives: 75.3 us -> 153 us
    psum x1 -> x2, blocking collectives: 75.3 us -> 153 us  [the longest x1 129 us: per_device(): lax.psum(lax.psum((short_part, skip_part), 'dp'), 'ctx')]
where the time goes in v1:
time: 1140 us; the launch traced here: 1130 us
  waiting for transfers between devices  870 us (76%)
  blocking collectives  153 us (13%)
  other arithmetic  50.9 us (4%)
  starting transfers between devices  22.9 us (2%)
  between operations  15.3 us (1%)
  matrix products  14.2 us (1%)
    ppermute x10, waiting for transfers between devices, swapped(): return lax.ppermute(value, axis, pairs)  797 us
    psum x1, blocking collectives, per_device(): lax.psum(lax.psum((short_part, skip_part), 'dp'), 'ctx')  129 us
    psum x1, waiting for transfers between devices, per_device(): filter_sum = lax.psum(filter_part, 'dp')  65 us
    psum x1, blocking collectives, per_device(): lax.psum((short_part, skip_part), 'dp')  24.7 us
  transfers between devices with their start and end apart: 13, of which 13 were waited for; matrix products, arithmetic and copies ran while one was open for 0% of the time, Pallas kernels for 0%

profile of v1, /device:TPU:2, one launch (start us, length us, event | category | flops | bytes accessed | tf_op | source)
XLA Modules:
  0.0 1134.9 jit_solution(6311240350361644040)
XLA Ops:
  8.0 3.8 collective-permute-start
  13.2 4.3 collective-permute-done
  23.9 2.4 collective-permute-start.1
  26.5 68.2 %collective-permute-done.1 = f32[2,2,128,1536]{3,2,1,0:T(8,128)} collective-permute-done((f32[2,2,128,1536]{3,2,1,0:T(8,128)}, f32[2,2,128,1536]{3,2,1,0:T(8,128)}, u32[]{:S(2)}, u32[]{:S(2)}) %collective-permute-start.1) | collective-permute-done | bytes 3145760 | tf_op jit(solution)/shard_map/ppermute | solution.py:13
  94.7 3.0 multiply_subtract_fusion.4
  100.3 67.9 %collective-permute-done.2 = f32[2,2,128,1536]{3,2,1,0:T(8,128)} collective-permute-done((f32[2,2,128,1536]{3,2,1,0:T(8,128)}, f32[2,2,128,1536]{3,2,1,0:T(8,128)}, u32[]{:S(2)}, u32[]{:S(2)}) %collective-permute-start.2) | collective-permute-done | bytes 3145760 | tf_op jit(solution)/shard_map/ppermute | solution.py:13
  168.2 3.1 multiply_subtract_fusion.3
  171.3 2.1 pad_maximum_fusion.2
  174.0 4.0 collective-permute-start.3
  178.2 135.4 %collective-permute-done.3 = f32[2,2,128,1536]{3,2,1,0:T(8,128)} collective-permute-done((f32[2,2,128,1536]{3,2,1,0:T(8,128)}, f32[2,2,128,1536]{3,2,1,0:T(8,128)}, u32[]{:S(2)}, u32[]{:S(2)}) %collective-permute-start.3) | collective-permute-done | bytes 3145760 | tf_op jit(solution)/shard_map/ppermute | solution.py:13
  313.6 3.6 multiply_subtract_fusion.2
  317.2 2.1 pad_maximum_fusion.3
  319.5 137.3 %collective-permute-done.4 = f32[2,2,128,1536]{3,2,1,0:T(8,128)} collective-permute-done((f32[2,2,128,1536]{3,2,1,0:T(8,128)}, f32[2,2,128,1536]{3,2,1,0:T(8,128)}, u32[]{:S(2)}, u32[]{:S(2)}) %collective-permute-start.4) | collective-permute-done | bytes 3145760 | tf_op jit(solution)/shard_map/ppermute | solution.py:13
  456.8 3.1 multiply_add_fusion.1
  459.9 2.0 pad_maximum_fusion.4
  462.7 69.4 %collective-permute-done.5 = f32[2,2,128,1536]{3,2,1,0:T(8,128)} collective-permute-done((f32[2,2,128,1536]{3,2,1,0:T(8,128)}, f32[2,2,128,1536]{3,2,1,0:T(8,128)}, u32[]{:S(2)}, u32[]{:S(2)}) %collective-permute-start.5) | collective-permute-done | bytes 3145760 | tf_op jit(solution)/shard_map/ppermute | solution.py:13
  532.1 3.5 fusion.2
  552.5 45.8 %collective-permute-done.6 = f32[2,2,128,1024]{3,2,1,0:T(8,128)} collective-permute-done((f32[2,2,128,1024]{3,2,1,0:T(8,128)}, f32[2,2,128,1024]{3,2,1,0:T(8,128)}, u32[]{:S(2)}, u32[]{:S(2)}) %collective-permute-start.6) | collective-permute-done | bytes 2097184 | tf_op jit(solution)/shard_map/ppermute | solution.py:13
  598.3 2.0 multiply_add_fusion.8
  602.8 2.1 collective-permute-start.7
  604.9 89.6 %collective-permute-done.7 = f32[2,2,128,1024]{3,2,1,0:T(8,128)} collective-permute-done((f32[2,2,128,1024]{3,2,1,0:T(8,128)}, f32[2,2,128,1024]{3,2,1,0:T(8,128)}, u32[]{:S(2)}, u32[]{:S(2)}) %collective-permute-start.7) | collective-permute-done | bytes 2097184 | tf_op jit(solution)/shard_map/ppermute | solution.py:13
  694.5 2.3 multiply_add_fusion.7
  698.2 3.7 collective-permute-start.8
  701.9 92.3 %collective-permute-done.8 = f32[2,2,128,1024]{3,2,1,0:T(8,128)} collective-permute-done((f32[2,2,128,1024]{3,2,1,0:T(8,128)S(1)}, f32[2,2,128,1024]{3,2,1,0:T(8,128)}, u32[]{:S(2)}, u32[]{:S(2)}) %collective-permute-start.8) | collective-permute-done | bytes 2097184 | tf_op jit(solution)/shard_map/ppermute | solution.py:13
  794.2 2.7 multiply_add_fusion.6
  799.3 46.3 %collective-permute-done.9 = f32[2,2,128,1024]{3,2,1,0:T(8,128)} collective-permute-done((f32[2,2,128,1024]{3,2,1,0:T(8,128)}, f32[2,2,128,1024]{3,2,1,0:T(8,128)}, u32[]{:S(2)}, u32[]{:S(2)}) %collective-permute-start.9) | collective-permute-done | bytes 2097184 | tf_op jit(solution)/shard_map/ppermute | solution.py:13
  847.8 3.3 collective-permute-start.10
  851.1 45.0 %collective-permute-done.10 = f32[2,2,128,1024]{3,2,1,0:T(8,128)S(1)} collective-permute-done((f32[2,2,128,1024]{3,2,1,0:T(8,128)S(1)}, f32[2,2,128,1024]{3,2,1,0:T(8,128)S(1)}, u32[]{:S(2)}, u32[]{:S(2)}) %collective-permute-start.10) | collective-permute-done | bytes 2097184 | tf_op jit(solution)/shard_map/ppermute | solution.py:13
  899.9 24.7 %all-reduce.2 = (f32[7,1536]{1,0:T(8,128)S(1)}, f32[512]{0:T(512)S(1)}) all-reduce(f32[7,1536]{1,0:T(8,128)S(1)} %stack.165, f32[512]{0:T(512)S(1)} %get-tuple-element.23), channel_id=1, replica_groups=mesh['dp'=8,'ctx'=32] {'dp'}, use_global_device_ids=true, to_apply=%region_7.8 | all-reduce | flops 11264 | bytes 90112 | tf_op jit(solution)/shard_map/psum | solution.py:179
  924.6 128.7 %all-reduce.1 = (f32[7,1536]{1,0:T(8,128)S(1)}, f32[512]{0:T(512)S(1)}) all-reduce(f32[7,1536]{1,0:T(8,128)S(1)} %get-tuple-element.21, f32[512]{0:T(512)S(1)} %get-tuple-element.22), channel_id=1, replica_groups=mesh['dp'=8,'ctx'=32] {'ctx'}, use_global_device_ids=true, to_apply=%region_8.9 | all-reduce | flops 11264 | bytes 90112 | tf_op jit(solution)/shard_map/psum | solution.py:179
  1056.5 3.4 collective-permute-done.11
  1061.3 65.0 %all-reduce.5.cloned.1.call-done = f32[128,512]{1,0:T(8,128)} async-done(((f32[128,512]{1,0:T(8,128)}), f32[128,512]{1,0:T(8,128)}) %all-reduce.5.cloned.1.call-update) | async-done | bytes 262160 | tf_op jit(solution)/shard_map/psum | solution.py:178
  (95 shorter events, 47.4 us)
Async XLA Ops:
  7.2 1119.2 %all-reduce.5.cloned.1.call-start = ((), (), s32[]{:S(2)}) async-start(), calls=%async_computation | async-start | bytes 524288 | tf_op jit(solution)/shard_map/psum | solution.py:178
  8.0 9.5 collective-permute-start
  18.6 0.9 copy-start.16
  19.5 1.4 copy-start.9
  19.5 1.1 copy-start.15
  19.6 1.3 copy-start.13
  20.9 0.9 copy-start.11
  20.9 1.1 copy-start.12
  23.9 70.8 %collective-permute-start.1 = (f32[2,2,128,1536]{3,2,1,0:T(8,128)}, f32[2,2,128,1536]{3,2,1,0:T(8,128)}, u32[]{:S(2)}, u32[]{:S(2)}) collective-permute-start(f32[2,2,128,1536]{3,2,1,0:T(8,128)} %pad_maximum_fusion), channel_id=1, source_target_pairs={{0,16},{1,17},{2,18},{3,19},{4,20},{5,21},{6,22},{7,23},{8,24},{9,... | collective-permute-start | bytes 9437192 | tf_op jit(solution)/shard_map/ppermute | solution.py:13
  97.7 2.1 copy-start.1
  99.9 68.4 %collective-permute-start.2 = (f32[2,2,128,1536]{3,2,1,0:T(8,128)}, f32[2,2,128,1536]{3,2,1,0:T(8,128)}, u32[]{:S(2)}, u32[]{:S(2)}) collective-permute-start(f32[2,2,128,1536]{3,2,1,0:T(8,128)} %pad_maximum_fusion.1), channel_id=1, source_target_pairs={{0,8},{1,9},{2,10},{3,11},{4,12},{5,13},{6,14},{7,15},{8,0},{9,1},... | collective-permute-start | bytes 9437192 | tf_op jit(solution)/shard_map/ppermute | solution.py:13
  171.3 2.3 copy-start.2
  171.3 2.7 copy-start.3
  174.0 139.6 %collective-permute-start.3 = (f32[2,2,128,1536]{3,2,1,0:T(8,128)}, f32[2,2,128,1536]{3,2,1,0:T(8,128)}, u32[]{:S(2)}, u32[]{:S(2)}) collective-permute-start(f32[2,2,128,1536]{3,2,1,0:T(8,128)} %pad_maximum_fusion.2), channel_id=1, source_target_pairs={{0,4},{1,5},{2,6},{3,7},{4,0},{5,1},{6,2},{7,3},{8,12},{9,13},{10,... | collective-permute-start | bytes 9437192 | tf_op jit(solution)/shard_map/ppermute | solution.py:13
  317.2 2.2 copy-start
  319.4 137.4 %collective-permute-start.4 = (f32[2,2,128,1536]{3,2,1,0:T(8,128)}, f32[2,2,128,1536]{3,2,1,0:T(8,128)}, u32[]{:S(2)}, u32[]{:S(2)}) collective-permute-start(f32[2,2,128,1536]{3,2,1,0:T(8,128)} %pad_maximum_fusion.3), channel_id=1, source_target_pairs={{0,2},{1,3},{2,0},{3,1},{4,6},{5,7},{6,4},{7,5},{8,10},{9,11},{10,... | collective-permute-start | bytes 9437192 | tf_op jit(solution)/shard_map/ppermute | solution.py:13
  459.9 2.1 copy-start.4
  459.9 2.7 copy-start.5
  462.6 69.5 %collective-permute-start.5 = (f32[2,2,128,1536]{3,2,1,0:T(8,128)}, f32[2,2,128,1536]{3,2,1,0:T(8,128)}, u32[]{:S(2)}, u32[]{:S(2)}) collective-permute-start(f32[2,2,128,1536]{3,2,1,0:T(8,128)} %pad_maximum_fusion.4), channel_id=1, source_target_pairs={{0,1},{1,0},{2,3},{3,2},{4,5},{5,4},{6,7},{7,6},{8,9},{9,8},{10,11... | collective-permute-start | bytes 9437192 | tf_op jit(solution)/shard_map/ppermute | solution.py:13
  552.2 46.1 %collective-permute-start.6 = (f32[2,2,128,1024]{3,2,1,0:T(8,128)}, f32[2,2,128,1024]{3,2,1,0:T(8,128)}, u32[]{:S(2)}, u32[]{:S(2)}) collective-permute-start(f32[2,2,128,1024]{3,2,1,0:T(8,128)} %pad_maximum_fusion.5), channel_id=1, source_target_pairs={{0,1},{1,0},{2,3},{3,2},{4,5},{5,4},{6,7},{7,6},{8,9},{9,8},{10,11... | collective-permute-start | bytes 6291464 | tf_op jit(solution)/shard_map/ppermute | solution.py:13
  600.4 1.0 copy-start.6
  602.8 91.7 %collective-permute-start.7 = (f32[2,2,128,1024]{3,2,1,0:T(8,128)}, f32[2,2,128,1024]{3,2,1,0:T(8,128)}, u32[]{:S(2)}, u32[]{:S(2)}) collective-permute-start(f32[2,2,128,1024]{3,2,1,0:T(8,128)} %pad_maximum_fusion.6), channel_id=1, source_target_pairs={{0,2},{1,3},{2,0},{3,1},{4,6},{5,7},{6,4},{7,5},{8,10},{9,11},{10,... | collective-permute-start | bytes 6291464 | tf_op jit(solution)/shard_map/ppermute | solution.py:13
  696.9 1.0 copy-start.7
  696.9 1.3 copy-start.8
  698.2 96.0 %collective-permute-start.8 = (f32[2,2,128,1024]{3,2,1,0:T(8,128)S(1)}, f32[2,2,128,1024]{3,2,1,0:T(8,128)}, u32[]{:S(2)}, u32[]{:S(2)}) collective-permute-start(f32[2,2,128,1024]{3,2,1,0:T(8,128)S(1)} %pad_maximum_fusion.7), channel_id=1, source_target_pairs={{0,4},{1,5},{2,6},{3,7},{4,0},{5,1},{6,2},{7,3},{8,12},{9,13},{10,... | collective-permute-start | bytes 6291464 | tf_op jit(solution)/shard_map/ppermute | solution.py:13
  798.3 47.2 %collective-permute-start.9 = (f32[2,2,128,1024]{3,2,1,0:T(8,128)}, f32[2,2,128,1024]{3,2,1,0:T(8,128)}, u32[]{:S(2)}, u32[]{:S(2)}) collective-permute-start(f32[2,2,128,1024]{3,2,1,0:T(8,128)} %pad_maximum_fusion.8), channel_id=1, source_target_pairs={{0,8},{1,9},{2,10},{3,11},{4,12},{5,13},{6,14},{7,15},{8,0},{9,1},... | collective-permute-start | bytes 6291464 | tf_op jit(solution)/shard_map/ppermute | solution.py:13
  847.8 48.3 %collective-permute-start.10 = (f32[2,2,128,1024]{3,2,1,0:T(8,128)S(1)}, f32[2,2,128,1024]{3,2,1,0:T(8,128)S(1)}, u32[]{:S(2)}, u32[]{:S(2)}) collective-permute-start(f32[2,2,128,1024]{3,2,1,0:T(8,128)S(1)} %pad_maximum_fusion.9), channel_id=1, source_target_pairs={{0,16},{1,17},{2,18},{3,19},{4,20},{5,21},{6,22},{7,23},{8,24},{9,... | collective-permute-start | bytes 6291464 | tf_op jit(solution)/shard_map/ppermute | solution.py:13
  896.7 1.1 copy-start.10
  896.7 1.2 copy-start.14
  896.8 1.2 copy-start.17
  896.8 1.2 copy-start.18
  1053.9 6.0 collective-permute-start.11
Sparse Core Ops, SparseCore 0:
  1056.6 69.7 all-reduce.4
